TPU v7x, 512 devices: a whole 4x4x16 slice. The times are simulated.
512 devices in a mesh: seq: 16 (over y, x), mp: 32 (over z, core).
Axes of the slice: x: 4, y: 4, z: 16, core: 2. Of those that a mesh axis runs over, the one named last changes fastest.
Arguments:
- q_proj: bfloat16 [4096, 8192], P('seq', 'mp'), may hold values from -6 to 6
- k_proj: bfloat16 [4096, 8192], P('seq', 'mp'), may hold values from -6 to 6
- v_proj: bfloat16 [4096, 8192], P('seq', 'mp'), may hold values from -6 to 6
- out_grad: bfloat16 [4096, 8192], P('seq', 'mp'), may hold values from -0.75 to 0.75
- out_weight: bfloat16 [8192, 8192], P('mp', 'seq'), may hold values from -0.0625 to 0.0625
- taps: float32 [7, 512], P(None, 'mp'), may hold values from -2.4 to 2.4
Outputs:
- grad_q: bfloat16 [4096, 8192], P('seq', 'mp')
- grad_k: bfloat16 [4096, 8192], P('seq', 'mp')
- grad_v: bfloat16 [4096, 8192], P('seq', 'mp')
- grad_weight: float32 [8192, 8192], P('mp', 'seq')
- grad_taps: float32 [7, 512], P(None, 'mp')
All inputs are finite; a program needn't handle non-finite values.
Results may differ from a plain program's by a relative error of at most 0.0029.
Values may be sent and summed in bfloat16 or wider, within the bound.
A program may use at most 64 MiB of HBM per device.

v0:
```python
import jax
import jax.numpy as jnp
from jax import lax
from jax.sharding import PartitionSpec as P

TAPS = 7
GROUP = 16


def passed_along(array, axis, by):
    count = lax.axis_size(axis)
    pairs = [(i, i + by) for i in range(count) if 0 <= i + by < count]
    return lax.ppermute(array, axis, pairs)


def shards(q_proj, k_proj, v_proj, out_grad, out_weight, taps):
    tokens, channels = q_proj.shape
    rim_rows = TAPS - 1
    q_full = q_proj.astype(jnp.float32)
    k_full = k_proj.astype(jnp.float32)
    v_full = v_proj.astype(jnp.float32)
    spread = jnp.broadcast_to(taps[:, :, None], (TAPS, taps.shape[1], GROUP)).reshape(
        TAPS, channels
    )
    tail_rows = jnp.stack([k_proj[tokens - rim_rows :], v_proj[tokens - rim_rows :]])
    before = passed_along(tail_rows, "seq", 1)
    keys_wide = jnp.concatenate([before[0], k_proj], 0).astype(jnp.float32)
    values_wide = jnp.concatenate([before[1], v_proj], 0).astype(jnp.float32)
    product = keys_wide * values_wide
    filtered = jnp.zeros((tokens, channels), jnp.float32)
    for offset in range(TAPS):
        filtered = (
            filtered + spread[offset] * product[rim_rows - offset : rim_rows - offset + tokens]
        )
    gated = (q_full * filtered).astype(jnp.bfloat16)
    seq_count, mp_count = (lax.axis_size("seq"), lax.axis_size("mp"))
    cores = mp_count // seq_count
    pairs = [
        (t * mp_count + cores * z + c, z * mp_count + cores * t + c)
        for t in range(seq_count)
        for z in range(seq_count)
        for c in range(cores)
    ]
    crossed = lax.ppermute(out_grad, ("seq", "mp"), pairs)
    tiles = lax.all_gather(crossed, "mp", axis=0)
    columns = (
        tiles.reshape(seq_count, cores, tokens, channels)
        .transpose(0, 2, 1, 3)
        .reshape(seq_count * tokens, cores * channels)
    )
    partial = lax.dot_general(
        columns, out_weight, (((1,), (1,)), ((), ())), preferred_element_type=jnp.float32
    )
    grad_gated = lax.psum_scatter(partial, "seq", scatter_dimension=0, tiled=True)
    grad_weight = lax.dot_general(
        lax.all_gather(gated, "seq", axis=0, tiled=True),
        columns,
        (((0,), (0,)), ((), ())),
        preferred_element_type=jnp.float32,
    )
    grad_q = (grad_gated * filtered).astype(jnp.bfloat16)
    grad_filtered = grad_gated * q_full
    following = passed_along(grad_filtered[:rim_rows], "seq", -1)
    grad_ext = jnp.concatenate([grad_filtered, following], 0)
    grad_product = jnp.zeros((tokens, channels), jnp.float32)
    for offset in range(TAPS):
        grad_product = grad_product + spread[offset] * grad_ext[offset : offset + tokens]
    grad_k = (grad_product * v_full).astype(jnp.bfloat16)
    grad_v = (grad_product * k_full).astype(jnp.bfloat16)
    filter_terms = jnp.stack(
        [
            jnp.sum(grad_filtered * product[rim_rows - offset : rim_rows - offset + tokens], 0)
            for offset in range(TAPS)
        ]
    )
    filter_local = filter_terms.reshape(TAPS, channels // GROUP, GROUP).sum(-1)
    grad_taps = lax.psum(filter_local, "seq")
    return (grad_q, grad_k, grad_v, grad_weight, grad_taps)


def solution(mesh):
    placed = (
        P("seq", "mp"),
        P("seq", "mp"),
        P("seq", "mp"),
        P("seq", "mp"),
        P("mp", "seq"),
        P(None, "mp"),
    )
    return jax.shard_map(
        shards,
        mesh=mesh,
        in_specs=placed,
        out_specs=(P("seq", "mp"), P("seq", "mp"), P("seq", "mp"), P("mp", "seq"), P(None, "mp")),
        check_vma=False,
    )
```

profile of v0, /device:TPU:32, one launch (start us, length us, event | category | flops | bytes accessed | tf_op | source)
XLA Modules:
  0.0 327.7 jit_solution(6569584320959466278)
XLA Ops:
  7.2 0.0 copy-start
  7.2 0.0 all-gather.6.cloned.1.call-start
  7.2 3.1 collective-permute-start
  10.3 12.5 %collective-permute-done = bf16[256,256]{1,0:T(8,128)(2,1)S(1)} collective-permute-done((bf16[256,256]{1,0:T(8,128)(2,1)}, bf16[256,256]{1,0:T(8,128)(2,1)S(1)}, u32[]{:S(2)}, u32[]{:S(2)}) %collective-permute-start) | collective-permute-done | bytes 131104 | tf_op jit(solution)/shard_map/ppermute | solution.py:44
  22.8 0.0 copy-start.5
  22.8 0.7 copy-done.5
  23.5 0.0 all-gather.6.cloned.1.call-update
  23.5 0.0 all-gather.4.cloned.1.call-start
  23.5 0.7 slice_bitcast_fusion.2
  24.3 1.3 collective-permute-start.1
  25.6 0.9 slice_bitcast_fusion.10
  26.5 0.1 broadcast_in_dim.44
  26.6 0.1 broadcast_in_dim.45
  26.7 0.1 broadcast_in_dim.42
  26.8 0.1 broadcast_in_dim.43
  26.8 0.1 broadcast_in_dim.40
  26.9 0.1 broadcast_in_dim.41
  27.0 0.1 broadcast_in_dim.38
  27.1 0.1 broadcast_in_dim.39
  27.1 0.1 broadcast_in_dim.36
  27.2 0.1 broadcast_in_dim.37
  27.3 0.1 broadcast_in_dim.34
  27.4 0.1 broadcast_in_dim.35
  27.4 0.1 broadcast_in_dim.32
  27.5 0.1 broadcast_in_dim.33
  27.6 0.0 collective-permute-done.1
  27.6 1.0 convert_multiply_fusion.2
  28.7 1.8 fusion
  30.5 0.0 all-gather.4.cloned.1.call-update
  30.5 0.0 reduce-scatter.2.cloned.1.call-start
  30.6 87.3 %all-gather.6.cloned.1.call-done = bf16[8192,256]{1,0:T(8,128)(2,1)} async-done(((bf16[256,256]{1,0:T(8,128)(2,1)}), bf16[8192,256]{1,0:T(8,128)(2,1)}) %all-gather.6.cloned.1.call-update) | async-done | bytes 4194320 | tf_op jit(solution)/shard_map/all_gather | solution.py:45
  117.8 8.0 %copy.12 = bf16[16,2,256,256]{2,0,3,1:T(8,128)(2,1)} copy(bf16[16,2,256,256]{3,2,1,0:T(8,128)(2,1)} %bitcast.36) | data formatting | bytes 8388608 | tf_op jit(solution)/shard_map/reshape | solution.py:47
  125.8 4.4 %copy.13 = bf16[64,8,16,256]{3,1,2,0:T(8,128)(2,1)S(1)} copy(bf16[64,8,16,256]{3,2,1,0:T(8,128)(2,1)} %bitcast.35) | data formatting | bytes 8388608
  130.2 0.0 copy-start.1
  130.2 2.0 copy-done.1
  132.2 0.0 copy-done
  132.2 3.2 fusion.19
  135.4 0.0 reduce-scatter.2.cloned.1.call-update
  135.4 0.0 copy-start.4
  135.4 0.0 copy-start.2
  135.4 0.0 copy-start.3
  135.5 43.0 %all-gather.4.cloned.1.call-done = bf16[4096,256]{1,0:T(8,128)(2,1)} async-done(((bf16[256,256]{1,0:T(8,128)(2,1)}), bf16[4096,256]{1,0:T(8,128)(2,1)}) %all-gather.4.cloned.1.call-update) | async-done | bytes 2097168 | tf_op jit(solution)/shard_map/all_gather | solution.py:56
  178.5 4.9 %fusion.20 = f32[256,512]{1,0:T(8,128)} fusion(bf16[4096,256]{1,0:T(8,128)(2,1)} %all-gather.4.cloned.1.call-done, bf16[4096,512]{0,1:T(8,128)(2,1)} %bitcast.34), kind=kOutput, calls=%fused_computation.61 | convolution fusion | flops 1073741824 | bytes 6815744 | tf_op jit(solution)/shard_map/dot_general | solution.py:55
  183.4 91.8 %reduce-scatter.2.cloned.1.call-done = f32[256,256]{1,0:T(8,128)} async-done(((f32[4096,256]{1,0:T(8,128)}), f32[256,256]{1,0:T(8,128)}) %reduce-scatter.2.cloned.1.call-update) | async-done | bytes 262160 | tf_op jit(solution)/shard_map/reduce_scatter | solution.py:54
  275.2 0.0 copy-done.4
  275.2 1.9 multiply_reduce_fusion
  277.1 1.3 collective-permute-start.2
  278.4 0.1 stack.36
  278.4 0.1 stack.37
  278.5 0.1 stack.38
  278.6 0.1 stack.39
  278.7 0.1 stack.40
  278.8 0.1 stack.41
  278.8 0.1 stack.42
  279.0 0.1 reduce_sum.79
  279.1 40.5 %psum.7 = f32[7,16]{1,0:T(8,128)} all-reduce(f32[7,16]{1,0:T(8,128)S(1)} %reduce_sum.79), channel_id=1, replica_groups=mesh['seq'=16,'mp'=32] {'seq'}, use_global_device_ids=true, to_apply=%region_9.0 | all-reduce | flops 112 | bytes 896 | tf_op jit(solution)/shard_map/psum | solution.py:77
  319.6 0.0 collective-permute-done.2
  319.6 0.0 copy-done.2
  319.6 0.9 multiply_convert_fusion
  320.5 0.0 copy-done.3
  320.5 0.7 multiply_convert_fusion.1
  (10 shorter events, 0.1 us)
Async XLA Ops:
  7.2 125.0 %copy-start = (bf16[256,512]{1,0:T(8,128)(2,1)S(1)}, bf16[256,512]{1,0:T(8,128)(2,1)}, u32[]{:S(2)}) copy-start(bf16[256,512]{1,0:T(8,128)(2,1)} %param.10) | copy-start | bytes 786436
  7.2 110.7 %all-gather.6.cloned.1.call-start = ((), (), s32[]{:S(2)}) async-start(), calls=%async_computation.3 | async-start | bytes 4325376 | tf_op jit(solution)/shard_map/all_gather | solution.py:45
  7.2 15.6 %collective-permute-start = (bf16[256,256]{1,0:T(8,128)(2,1)}, bf16[256,256]{1,0:T(8,128)(2,1)S(1)}, u32[]{:S(2)}, u32[]{:S(2)}) collective-permute-start(bf16[256,256]{1,0:T(8,128)(2,1)} %param.9), channel_id=1, source_target_pairs={{0,0},{1,1},{2,32},{3,33},{4,64},{5,65},{6,96},{7,97},{8,128},{9,1... | collective-permute-start | bytes 393224 | tf_op jit(solution)/shard_map/ppermute | solution.py:44
  22.8 0.7 copy-start.5
  23.5 155.0 %all-gather.4.cloned.1.call-start = ((), (), s32[]{:S(2)}) async-start(), calls=%async_computation.2 | async-start | bytes 2228224 | tf_op jit(solution)/shard_map/all_gather | solution.py:56
  24.3 3.3 %collective-permute-start.1 = (bf16[2,6,256]{2,1,0:T(8,128)(2,1)S(1)}, bf16[2,6,256]{2,1,0:T(8,128)(2,1)S(1)}, u32[]{:S(2)}, u32[]{:S(2)}) collective-permute-start(bf16[2,6,256]{2,1,0:T(8,128)(2,1)S(1)} %pad_maximum_fusion.1), channel_id=1, source_target_pairs={{0,32},{32,64},{64,96},{96,128},{128,160},{160,192},{192,224},{224... | collective-permute-start | bytes 18440 | tf_op jit(solution)/shard_map/ppermute | solution.py:13
  30.5 244.7 %reduce-scatter.2.cloned.1.call-start = ((), (), s32[]{:S(2)}) async-start(), calls=%async_computation.1 | async-start | bytes 4456448 | tf_op jit(solution)/shard_map/reduce_scatter | solution.py:54
  130.2 2.0 copy-start.1
  135.4 139.8 %copy-start.4 = (bf16[256,256]{1,0:T(8,128)(2,1)S(1)}, bf16[256,256]{1,0:T(8,128)(2,1)}, u32[]{:S(2)}) copy-start(bf16[256,256]{1,0:T(8,128)(2,1)} %param.6) | copy-start | bytes 393220
  135.4 184.1 %copy-start.2 = (bf16[256,256]{1,0:T(8,128)(2,1)S(1)}, bf16[256,256]{1,0:T(8,128)(2,1)}, u32[]{:S(2)}) copy-start(bf16[256,256]{1,0:T(8,128)(2,1)} %param.7) | copy-start | bytes 393220
  135.4 185.0 %copy-start.3 = (bf16[256,256]{1,0:T(8,128)(2,1)S(1)}, bf16[256,256]{1,0:T(8,128)(2,1)}, u32[]{:S(2)}) copy-start(bf16[256,256]{1,0:T(8,128)(2,1)} %param.8) | copy-start | bytes 393220
  277.1 42.5 %collective-permute-start.2 = (f32[6,256]{1,0:T(8,128)S(1)}, f32[6,256]{1,0:T(8,128)S(1)}, u32[]{:S(2)}, u32[]{:S(2)}) collective-permute-start(f32[6,256]{1,0:T(8,128)S(1)} %slice.158), channel_id=1, source_target_pairs={{32,0},{64,32},{96,64},{128,96},{160,128},{192,160},{224,192},{256... | collective-permute-start | bytes 18440 | tf_op jit(solution)/shard_map/ppermute | solution.py:13
Sparse Core Ops, SparseCore 0:
  23.6 94.1 all-gather.5
  121.4 57.0 all-gather.3
  182.7 92.4 reduce-scatter.1
where the time goes:
time: 328 us
  waiting for transfers between devices  235 us (72%)
  blocking collectives  40.5 us (12%)
  local copies, waits for them, and re-layouts  18.3 us (6%)
  between operations  13.9 us (4%)
  matrix products  8.15 us (2%)
  other arithmetic  6.39 us (2%)
  starting transfers between devices  5.76 us (2%)
    reduce_scatter x1, waiting for transfers between devices, shards(): lax.psum_scatter(partial, 'seq', scatter_dimension=0, tiled=True)  91.8 us
    all_gather x1, waiting for transfers between devices, shards(): tiles = lax.all_gather(crossed, 'mp', axis=0)  87.3 us
    all_gather x1, waiting for transfers between devices, shards(): lax.all_gather(gated, 'seq', axis=0, tiled=True)  43 us
    psum x1, blocking collectives, shards(): grad_taps = lax.psum(filter_local, 'seq')  40.5 us
    ppermute x1, waiting for transfers between devices, shards(): crossed = lax.ppermute(out_grad, ('seq', 'mp'), pairs)  12.5 us
    reshape x1, local copies, waits for them, and re-layouts, shards(): tiles.reshape(seq_count, cores, tokens, channels).transpose(0, 2, 1, 3)  7.96 us
    unnamed x19, local copies, waits for them, and re-layouts  7.08 us
  transfers between devices with their start and end apart: 6, of which 4 were waited for; matrix products, arithmetic and copies ran while one was open for 8% of the time, Pallas kernels for 0%

commit v1 on v0

--- a/solution.py
+++ b/solution.py
@@ -5,6 +5,27 @@
 
 TAPS = 7
 GROUP = 16
+
+
+def collect(value, axis, dim):
+    size, position, width = (lax.axis_size(axis), lax.axis_index(axis), value.shape[dim])
+    right = [(i, (i + 1) % size) for i in range(size)]
+    left = [(i, (i - 1) % size) for i in range(size)]
+    whole = jnp.zeros((*value.shape[:dim], size * width, *value.shape[dim + 1 :]), value.dtype)
+    whole = lax.dynamic_update_slice_in_dim(whole, value, position * width, axis=dim)
+    from_left = from_right = value
+    half = size // 2
+    for hop in range(1, half + 1):
+        from_left = lax.ppermute(from_left, axis, right)
+        whole = lax.dynamic_update_slice_in_dim(
+            whole, from_left, (position - hop) % size * width, axis=dim
+        )
+        if hop < size - half:
+            from_right = lax.ppermute(from_right, axis, left)
+            whole = lax.dynamic_update_slice_in_dim(
+                whole, from_right, (position + hop) % size * width, axis=dim
+            )
+    return whole
 
 
 def passed_along(array, axis, by):
@@ -53,7 +74,7 @@
     )
     grad_gated = lax.psum_scatter(partial, "seq", scatter_dimension=0, tiled=True)
     grad_weight = lax.dot_general(
-        lax.all_gather(gated, "seq", axis=0, tiled=True),
+        collect(gated, "seq", 0),
         columns,
         (((0,), (0,)), ((), ())),
         preferred_element_type=jnp.float32,

time: 328 us -> 286 us (0.87)
  waiting for transfers between devices: 235 us -> 126 us
  starting transfers between devices: 5.76 us -> 74.9 us
    reduce_scatter x1, waiting for transfers between devices: 91.8 us -> 0.02 us  [shards(): lax.psum_scatter(partial, 'seq', scatter_dimension=0, tiled=True)]
    ppermute x0 -> x15, starting transfers between devices: none -> 67.1 us  [the longest x7 49.6 us: collect(): from_right = lax.ppermute(from_right, axis, left)]
    all_gather x1 -> x0, waiting for transfers between devices: 43 us -> none  [shards(): lax.all_gather(gated, 'seq', axis=0, tiled=True)]
    ppermute x0 -> x15, waiting for transfers between devices: none -> 18.6 us  [the longest x8 18.6 us: collect(): from_left = lax.ppermute(from_left, axis, right)]
    all_gather x1, waiting for transfers between devices: 87.3 us -> 94.4 us  [shards(): tiles = lax.all_gather(crossed, 'mp', axis=0)]
    unnamed x19 -> x41, local copies, waits for them, and re-layouts: 7.08 us -> 8.05 us
  transfers between devices with their start and end apart: 6 -> 20, of which waited for: 4 -> 11; matrix products, arithmetic and copies ran while one was open for 8% -> 3% of each run, Pallas kernels for 0% -> 0%
where the time goes in v1:
time: 286 us; the launch traced here: 285 us
  waiting for transfers between devices  126 us (44%)
  starting transfers between devices  74.9 us (26%)
  blocking collectives  38.7 us (14%)
  local copies, waits for them, and re-layouts  18.9 us (7%)
  between operations  14.8 us (5%)
  matrix products  7.67 us (3%)
  other arithmetic  3.88 us (1%)
    all_gather x1, waiting for transfers between devices, shards(): tiles = lax.all_gather(crossed, 'mp', axis=0)  94.4 us
    ppermute x7, starting transfers between devices, collect(): from_right = lax.ppermute(from_right, axis, left)  49.6 us
    psum x1, blocking collectives, shards(): grad_taps = lax.psum(filter_local, 'seq')  38.7 us
    ppermute x8, waiting for transfers between devices, collect(): from_left = lax.ppermute(from_left, axis, right)  18.6 us
    ppermute x8, starting transfers between devices, collect(): from_left = lax.ppermute(from_left, axis, right)  17.6 us
    ppermute x1, waiting for transfers between devices, shards(): crossed = lax.ppermute(out_grad, ('seq', 'mp'), pairs)  12.4 us
    unnamed x41, local copies, waits for them, and re-layouts  8.05 us
    reshape x1, local copies, waits for them, and re-layouts, shards(): tiles.reshape(seq_count, cores, tokens, channels).transpose(0, 2, 1, 3)  7.93 us
  transfers between devices with their start and end apart: 20, of which 11 were waited for; matrix products, arithmetic and copies ran while one was open for 3% of the time, Pallas kernels for 0%

profile of v1, /device:TPU:32, one launch (start us, length us, event | category | flops | bytes accessed | tf_op | source)
XLA Modules:
  0.0 284.6 jit_solution(17963590705045483555)
XLA Ops:
  7.2 3.1 %collective-permute-start = (bf16[256,256]{1,0:T(8,128)(2,1)}, bf16[256,256]{1,0:T(8,128)(2,1)S(1)}, u32[]{:S(2)}, u32[]{:S(2)}) collective-permute-start(bf16[256,256]{1,0:T(8,128)(2,1)} %param.9), channel_id=1, source_target_pairs={{0,0},{1,1},{2,32},{3,33},{4,64},{5,65},{6,96},{7,97},{8,128},{9,1... | collective-permute-start | bytes 393224 | tf_op jit(solution)/shard_map/ppermute | solution.py:65
  10.3 12.4 %collective-permute-done = bf16[256,256]{1,0:T(8,128)(2,1)S(1)} collective-permute-done((bf16[256,256]{1,0:T(8,128)(2,1)}, bf16[256,256]{1,0:T(8,128)(2,1)S(1)}, u32[]{:S(2)}, u32[]{:S(2)}) %collective-permute-start) | collective-permute-done | bytes 131104 | tf_op jit(solution)/shard_map/ppermute | solution.py:65
  22.7 0.7 copy-done.5
  23.4 94.4 %all-gather.3.cloned.1.call-done = bf16[8192,256]{1,0:T(8,128)(2,1)} async-done(((bf16[256,256]{1,0:T(8,128)(2,1)}), bf16[8192,256]{1,0:T(8,128)(2,1)}) %all-gather.3.cloned.1.call-update) | async-done | bytes 4194320 | tf_op jit(solution)/shard_map/all_gather | solution.py:66
  117.9 7.9 %copy.12 = bf16[16,2,256,256]{2,0,3,1:T(8,128)(2,1)} copy(bf16[16,2,256,256]{3,2,1,0:T(8,128)(2,1)} %bitcast.36) | data formatting | bytes 8388608 | tf_op jit(solution)/shard_map/reshape | solution.py:68
  125.8 4.4 %copy.13 = bf16[64,8,16,256]{3,1,2,0:T(8,128)(2,1)S(1)} copy(bf16[64,8,16,256]{3,2,1,0:T(8,128)(2,1)} %bitcast.35) | data formatting | bytes 8388608
  130.2 2.0 copy-done.1
  132.2 3.3 %fusion.20 = f32[4096,256]{1,0:T(8,128)} fusion(bf16[4096,512]{0,1:T(8,128)(2,1)S(1)} %bitcast.33, bf16[256,512]{1,0:T(8,128)(2,1)S(1)} %copy-done), kind=kOutput, calls=%fused_computation.76 | convolution fusion | flops 1073741824 | bytes 8650752 | tf_op jit(solution)/shard_map/dot_general | solution.py:72
  135.5 0.9 copy-done.2
  136.4 3.4 %collective-permute-start.1 = (bf16[2,6,256]{2,1,0:T(8,128)(2,1)S(1)}, bf16[2,6,256]{2,1,0:T(8,128)(2,1)S(1)}, u32[]{:S(2)}, u32[]{:S(2)}) collective-permute-start(bf16[2,6,256]{2,1,0:T(8,128)(2,1)S(1)} %pad_maximum_fusion.1), channel_id=1, source_target_pairs={{0,32},{32,64},{64,96},{96,128},{128,160},{160,192},{192,224},{224... | collective-permute-start | bytes 18440 | tf_op jit(solution)/shard_map/ppermute | solution.py:34
  139.9 0.1 broadcast_in_dim.47
  139.9 0.1 broadcast_in_dim.48
  140.1 0.1 broadcast_in_dim.46
  140.2 0.1 broadcast_in_dim.43
  140.2 0.1 broadcast_in_dim.44
  140.3 0.1 broadcast_in_dim.41
  140.4 0.1 broadcast_in_dim.42
  140.5 0.1 broadcast_in_dim.39
  140.6 0.1 broadcast_in_dim.40
  140.7 0.1 broadcast_in_dim.37
  140.7 0.1 broadcast_in_dim.38
  140.8 0.1 broadcast_in_dim.35
  140.9 0.1 broadcast_in_dim.36
  141.0 0.2 collective-permute-done.1
  141.3 0.1 broadcast_in_dim.49
  141.4 0.2 constant_dynamic-update-slice_fusion.22
  141.7 4.2 %collective-permute-start.3 = (bf16[256,256]{1,0:T(8,128)(2,1)S(1)}, bf16[256,256]{1,0:T(8,128)(2,1)}, u32[]{:S(2)}, u32[]{:S(2)}) collective-permute-start(bf16[256,256]{1,0:T(8,128)(2,1)S(1)} %get-tuple-element.14), channel_id=1, source_target_pairs={{0,32},{32,64},{64,96},{96,128},{128,160},{160,192},{192,224},{224... | collective-permute-start | bytes 393224 | tf_op jit(solution)/shard_map/ppermute | solution.py:19
  145.9 5.3 %collective-permute-start.4 = (bf16[256,256]{1,0:T(8,128)(2,1)S(1)}, bf16[256,256]{1,0:T(8,128)(2,1)S(1)}, u32[]{:S(2)}, u32[]{:S(2)}) collective-permute-start(bf16[256,256]{1,0:T(8,128)(2,1)S(1)} %get-tuple-element.14), channel_id=1, source_target_pairs={{0,480},{32,0},{64,32},{96,64},{128,96},{160,128},{192,160},{224,1... | collective-permute-start | bytes 393224 | tf_op jit(solution)/shard_map/ppermute | solution.py:24
  151.5 0.8 collective-permute-done.3
  152.4 1.9 collective-permute-start.5
  154.3 7.3 %collective-permute-start.6 = (bf16[256,256]{1,0:T(8,128)(2,1)S(1)}, bf16[256,256]{1,0:T(8,128)(2,1)S(1)}, u32[]{:S(2)}, u32[]{:S(2)}) collective-permute-start(bf16[256,256]{1,0:T(8,128)(2,1)S(1)} %collective-permute-done.4), channel_id=1, source_target_pairs={{0,480},{32,0},{64,32},{96,64},{128,96},{160,128},{192,160},{224,1... | collective-permute-start | bytes 393224 | tf_op jit(solution)/shard_map/ppermute | solution.py:24
  161.6 0.9 constant_dynamic-update-slice_fusion.21
  162.6 1.0 collective-permute-done.5
  163.6 1.9 collective-permute-start.7
  165.5 7.5 %collective-permute-start.8 = (bf16[256,256]{1,0:T(8,128)(2,1)S(1)}, bf16[256,256]{1,0:T(8,128)(2,1)S(1)}, u32[]{:S(2)}, u32[]{:S(2)}) collective-permute-start(bf16[256,256]{1,0:T(8,128)(2,1)S(1)} %collective-permute-done.6), channel_id=1, source_target_pairs={{0,480},{32,0},{64,32},{96,64},{128,96},{160,128},{192,160},{224,1... | collective-permute-start | bytes 393224 | tf_op jit(solution)/shard_map/ppermute | solution.py:24
  173.1 1.9 collective-permute-done.7
  175.0 1.9 collective-permute-start.9
  176.9 7.3 %collective-permute-start.10 = (bf16[256,256]{1,0:T(8,128)(2,1)S(1)}, bf16[256,256]{1,0:T(8,128)(2,1)S(1)}, u32[]{:S(2)}, u32[]{:S(2)}) collective-permute-start(bf16[256,256]{1,0:T(8,128)(2,1)S(1)} %collective-permute-done.8), channel_id=1, source_target_pairs={{0,480},{32,0},{64,32},{96,64},{128,96},{160,128},{192,160},{224,1... | collective-permute-start | bytes 393224 | tf_op jit(solution)/shard_map/ppermute | solution.py:24
  184.3 1.6 collective-permute-done.9
  185.9 1.9 collective-permute-start.11
  187.9 7.2 %collective-permute-start.12 = (bf16[256,256]{1,0:T(8,128)(2,1)S(1)}, bf16[256,256]{1,0:T(8,128)(2,1)S(1)}, u32[]{:S(2)}, u32[]{:S(2)}) collective-permute-start(bf16[256,256]{1,0:T(8,128)(2,1)S(1)} %collective-permute-done.10), channel_id=1, source_target_pairs={{0,480},{32,0},{64,32},{96,64},{128,96},{160,128},{192,160},{224,1... | collective-permute-start | bytes 393224 | tf_op jit(solution)/shard_map/ppermute | solution.py:24
  195.2 1.6 collective-permute-done.11
  196.8 1.9 collective-permute-start.13
  198.7 7.2 %collective-permute-start.14 = (bf16[256,256]{1,0:T(8,128)(2,1)S(1)}, bf16[256,256]{1,0:T(8,128)(2,1)S(1)}, u32[]{:S(2)}, u32[]{:S(2)}) collective-permute-start(bf16[256,256]{1,0:T(8,128)(2,1)S(1)} %collective-permute-done.12), channel_id=1, source_target_pairs={{0,480},{32,0},{64,32},{96,64},{128,96},{160,128},{192,160},{224,1... | collective-permute-start | bytes 393224 | tf_op jit(solution)/shard_map/ppermute | solution.py:24
  206.0 1.0 collective-permute-done.13
  207.0 1.9 collective-permute-start.15
  209.0 7.6 %collective-permute-start.16 = (bf16[256,256]{1,0:T(8,128)(2,1)S(1)}, bf16[256,256]{1,0:T(8,128)(2,1)S(1)}, u32[]{:S(2)}, u32[]{:S(2)}) collective-permute-start(bf16[256,256]{1,0:T(8,128)(2,1)S(1)} %collective-permute-done.14), channel_id=1, source_target_pairs={{0,480},{32,0},{64,32},{96,64},{128,96},{160,128},{192,160},{224,1... | collective-permute-start | bytes 393224 | tf_op jit(solution)/shard_map/ppermute | solution.py:24
  216.6 1.9 collective-permute-done.15
  218.5 1.9 collective-permute-start.17
  220.4 8.7 %collective-permute-done.17 = bf16[256,256]{1,0:T(8,128)(2,1)S(1)} collective-permute-done((bf16[256,256]{1,0:T(8,128)(2,1)S(1)}, bf16[256,256]{1,0:T(8,128)(2,1)S(1)}, u32[]{:S(2)}, u32[]{:S(2)}) %collective-permute-start.17) | collective-permute-done | bytes 131104 | tf_op jit(solution)/shard_map/ppermute | solution.py:19
  229.2 4.4 %fusion.21 = f32[256,512]{1,0:T(8,128)} fusion(bf16[4096,256]{1,0:T(8,128)(2,1)S(1)} %constant_dynamic-update-slice_fusion.7, bf16[4096,512]{0,1:T(8,128)(2,1)} %bitcast.34), kind=kOutput, calls=%fused_computation.77 | convolution fusion | flops 1073741824 | bytes 6815744 | tf_op jit(solution)/shard_map/dot_general | solution.py:76
  233.6 1.9 multiply_reduce_fusion
  235.5 1.3 collective-permute-start.2
  236.8 0.1 stack.36
  236.9 0.1 stack.37
  236.9 0.1 stack.38
  237.0 0.1 stack.39
  237.1 0.1 stack.40
  237.2 0.1 stack.41
  237.2 0.1 stack.42
  237.4 0.1 reduce_sum.79
  237.5 38.7 %psum.7 = f32[7,16]{1,0:T(8,128)} all-reduce(f32[7,16]{1,0:T(8,128)S(1)} %reduce_sum.79), channel_id=1, replica_groups=mesh['seq'=16,'mp'=32] {'seq'}, use_global_device_ids=true, to_apply=%region_9.10 | all-reduce | flops 112 | bytes 896 | tf_op jit(solution)/shard_map/psum | solution.py:98
  276.2 0.9 multiply_convert_fusion
  277.1 0.7 multiply_convert_fusion.1
  (72 shorter events, 0.7 us)
Async XLA Ops:
  7.2 125.0 %copy-start = (bf16[256,512]{1,0:T(8,128)(2,1)S(1)}, bf16[256,512]{1,0:T(8,128)(2,1)}, u32[]{:S(2)}) copy-start(bf16[256,512]{1,0:T(8,128)(2,1)} %param.10) | copy-start | bytes 786436
  7.2 110.7 %all-gather.3.cloned.1.call-start = ((), (), s32[]{:S(2)}) async-start(), calls=%async_computation.2 | async-start | bytes 4325376 | tf_op jit(solution)/shard_map/all_gather | solution.py:66
  7.2 15.5 %collective-permute-start = (bf16[256,256]{1,0:T(8,128)(2,1)}, bf16[256,256]{1,0:T(8,128)(2,1)S(1)}, u32[]{:S(2)}, u32[]{:S(2)}) collective-permute-start(bf16[256,256]{1,0:T(8,128)(2,1)} %param.9), channel_id=1, source_target_pairs={{0,0},{1,1},{2,32},{3,33},{4,64},{5,65},{6,96},{7,97},{8,128},{9,1... | collective-permute-start | bytes 393224 | tf_op jit(solution)/shard_map/ppermute | solution.py:65
  22.7 0.7 copy-start.5
  23.4 210.2 %reduce-scatter.2.cloned.1.call-start = ((), (), s32[]{:S(2)}) async-start(), calls=%async_computation.1 | async-start | bytes 4456448 | tf_op jit(solution)/shard_map/reduce_scatter | solution.py:75
  130.2 2.0 copy-start.1
  135.4 0.9 copy-start.2
  135.4 1.0 copy-start.3
  135.4 4.4 %copy-start.16 = (f32[7,16]{1,0:T(8,128)S(1)}, f32[7,16]{1,0:T(8,128)}, u32[]{:S(2)}) copy-start(f32[7,16]{1,0:T(8,128)} %param.11) | copy-start | bytes 1348
  136.4 5.0 %copy-start.4 = (bf16[256,256]{1,0:T(8,128)(2,1)S(1)}, bf16[256,256]{1,0:T(8,128)(2,1)}, u32[]{:S(2)}) copy-start(bf16[256,256]{1,0:T(8,128)(2,1)} %param.6) | copy-start | bytes 393220
  136.4 4.8 %collective-permute-start.1 = (bf16[2,6,256]{2,1,0:T(8,128)(2,1)S(1)}, bf16[2,6,256]{2,1,0:T(8,128)(2,1)S(1)}, u32[]{:S(2)}, u32[]{:S(2)}) collective-permute-start(bf16[2,6,256]{2,1,0:T(8,128)(2,1)S(1)} %pad_maximum_fusion.1), channel_id=1, source_target_pairs={{0,32},{32,64},{64,96},{96,128},{128,160},{160,192},{192,224},{224... | collective-permute-start | bytes 18440 | tf_op jit(solution)/shard_map/ppermute | solution.py:34
  140.3 1.3 copy-start.6
  140.5 1.2 copy-start.8
  140.6 1.0 copy-start.10
  140.8 0.9 copy-start.12
  141.0 0.8 copy-start.14
  141.7 10.6 %collective-permute-start.3 = (bf16[256,256]{1,0:T(8,128)(2,1)S(1)}, bf16[256,256]{1,0:T(8,128)(2,1)}, u32[]{:S(2)}, u32[]{:S(2)}) collective-permute-start(bf16[256,256]{1,0:T(8,128)(2,1)S(1)} %get-tuple-element.14), channel_id=1, source_target_pairs={{0,32},{32,64},{64,96},{96,128},{128,160},{160,192},{192,224},{224... | collective-permute-start | bytes 393224 | tf_op jit(solution)/shard_map/ppermute | solution.py:19
  145.9 8.3 %collective-permute-start.4 = (bf16[256,256]{1,0:T(8,128)(2,1)S(1)}, bf16[256,256]{1,0:T(8,128)(2,1)S(1)}, u32[]{:S(2)}, u32[]{:S(2)}) collective-permute-start(bf16[256,256]{1,0:T(8,128)(2,1)S(1)} %get-tuple-element.14), channel_id=1, source_target_pairs={{0,480},{32,0},{64,32},{96,64},{128,96},{160,128},{192,160},{224,1... | collective-permute-start | bytes 393224 | tf_op jit(solution)/shard_map/ppermute | solution.py:24
  152.4 11.2 %collective-permute-start.5 = (bf16[256,256]{1,0:T(8,128)(2,1)}, bf16[256,256]{1,0:T(8,128)(2,1)S(1)}, u32[]{:S(2)}, u32[]{:S(2)}) collective-permute-start(bf16[256,256]{1,0:T(8,128)(2,1)} %collective-permute-done.3), channel_id=1, source_target_pairs={{0,32},{32,64},{64,96},{96,128},{128,160},{160,192},{192,224},{224... | collective-permute-start | bytes 393224 | tf_op jit(solution)/shard_map/ppermute | solution.py:19
  154.3 11.2 %collective-permute-start.6 = (bf16[256,256]{1,0:T(8,128)(2,1)S(1)}, bf16[256,256]{1,0:T(8,128)(2,1)S(1)}, u32[]{:S(2)}, u32[]{:S(2)}) collective-permute-start(bf16[256,256]{1,0:T(8,128)(2,1)S(1)} %collective-permute-done.4), channel_id=1, source_target_pairs={{0,480},{32,0},{64,32},{96,64},{128,96},{160,128},{192,160},{224,1... | collective-permute-start | bytes 393224 | tf_op jit(solution)/shard_map/ppermute | solution.py:24
  163.6 11.4 %collective-permute-start.7 = (bf16[256,256]{1,0:T(8,128)(2,1)S(1)}, bf16[256,256]{1,0:T(8,128)(2,1)S(1)}, u32[]{:S(2)}, u32[]{:S(2)}) collective-permute-start(bf16[256,256]{1,0:T(8,128)(2,1)S(1)} %collective-permute-done.5), channel_id=1, source_target_pairs={{0,32},{32,64},{64,96},{96,128},{128,160},{160,192},{192,224},{224... | collective-permute-start | bytes 393224 | tf_op jit(solution)/shard_map/ppermute | solution.py:19
  165.5 11.3 %collective-permute-start.8 = (bf16[256,256]{1,0:T(8,128)(2,1)S(1)}, bf16[256,256]{1,0:T(8,128)(2,1)S(1)}, u32[]{:S(2)}, u32[]{:S(2)}) collective-permute-start(bf16[256,256]{1,0:T(8,128)(2,1)S(1)} %collective-permute-done.6), channel_id=1, source_target_pairs={{0,480},{32,0},{64,32},{96,64},{128,96},{160,128},{192,160},{224,1... | collective-permute-start | bytes 393224 | tf_op jit(solution)/shard_map/ppermute | solution.py:24
  175.0 11.0 %collective-permute-start.9 = (bf16[256,256]{1,0:T(8,128)(2,1)S(1)}, bf16[256,256]{1,0:T(8,128)(2,1)S(1)}, u32[]{:S(2)}, u32[]{:S(2)}) collective-permute-start(bf16[256,256]{1,0:T(8,128)(2,1)S(1)} %collective-permute-done.7), channel_id=1, source_target_pairs={{0,32},{32,64},{64,96},{96,128},{128,160},{160,192},{192,224},{224... | collective-permute-start | bytes 393224 | tf_op jit(solution)/shard_map/ppermute | solution.py:19
  176.9 11.0 %collective-permute-start.10 = (bf16[256,256]{1,0:T(8,128)(2,1)S(1)}, bf16[256,256]{1,0:T(8,128)(2,1)S(1)}, u32[]{:S(2)}, u32[]{:S(2)}) collective-permute-start(bf16[256,256]{1,0:T(8,128)(2,1)S(1)} %collective-permute-done.8), channel_id=1, source_target_pairs={{0,480},{32,0},{64,32},{96,64},{128,96},{160,128},{192,160},{224,1... | collective-permute-start | bytes 393224 | tf_op jit(solution)/shard_map/ppermute | solution.py:24
  185.9 10.8 %collective-permute-start.11 = (bf16[256,256]{1,0:T(8,128)(2,1)S(1)}, bf16[256,256]{1,0:T(8,128)(2,1)S(1)}, u32[]{:S(2)}, u32[]{:S(2)}) collective-permute-start(bf16[256,256]{1,0:T(8,128)(2,1)S(1)} %collective-permute-done.9), channel_id=1, source_target_pairs={{0,32},{32,64},{64,96},{96,128},{128,160},{160,192},{192,224},{224... | collective-permute-start | bytes 393224 | tf_op jit(solution)/shard_map/ppermute | solution.py:19
  187.9 10.8 %collective-permute-start.12 = (bf16[256,256]{1,0:T(8,128)(2,1)S(1)}, bf16[256,256]{1,0:T(8,128)(2,1)S(1)}, u32[]{:S(2)}, u32[]{:S(2)}) collective-permute-start(bf16[256,256]{1,0:T(8,128)(2,1)S(1)} %collective-permute-done.10), channel_id=1, source_target_pairs={{0,480},{32,0},{64,32},{96,64},{128,96},{160,128},{192,160},{224,1... | collective-permute-start | bytes 393224 | tf_op jit(solution)/shard_map/ppermute | solution.py:24
  196.8 10.3 %collective-permute-start.13 = (bf16[256,256]{1,0:T(8,128)(2,1)S(1)}, bf16[256,256]{1,0:T(8,128)(2,1)S(1)}, u32[]{:S(2)}, u32[]{:S(2)}) collective-permute-start(bf16[256,256]{1,0:T(8,128)(2,1)S(1)} %collective-permute-done.11), channel_id=1, source_target_pairs={{0,32},{32,64},{64,96},{96,128},{128,160},{160,192},{192,224},{224... | collective-permute-start | bytes 393224 | tf_op jit(solution)/shard_map/ppermute | solution.py:19
  198.7 10.3 %collective-permute-start.14 = (bf16[256,256]{1,0:T(8,128)(2,1)S(1)}, bf16[256,256]{1,0:T(8,128)(2,1)S(1)}, u32[]{:S(2)}, u32[]{:S(2)}) collective-permute-start(bf16[256,256]{1,0:T(8,128)(2,1)S(1)} %collective-permute-done.12), channel_id=1, source_target_pairs={{0,480},{32,0},{64,32},{96,64},{128,96},{160,128},{192,160},{224,1... | collective-permute-start | bytes 393224 | tf_op jit(solution)/shard_map/ppermute | solution.py:24
  207.0 11.4 %collective-permute-start.15 = (bf16[256,256]{1,0:T(8,128)(2,1)S(1)}, bf16[256,256]{1,0:T(8,128)(2,1)S(1)}, u32[]{:S(2)}, u32[]{:S(2)}) collective-permute-start(bf16[256,256]{1,0:T(8,128)(2,1)S(1)} %collective-permute-done.13), channel_id=1, source_target_pairs={{0,32},{32,64},{64,96},{96,128},{128,160},{160,192},{192,224},{224... | collective-permute-start | bytes 393224 | tf_op jit(solution)/shard_map/ppermute | solution.py:19
  209.0 11.4 %collective-permute-start.16 = (bf16[256,256]{1,0:T(8,128)(2,1)S(1)}, bf16[256,256]{1,0:T(8,128)(2,1)S(1)}, u32[]{:S(2)}, u32[]{:S(2)}) collective-permute-start(bf16[256,256]{1,0:T(8,128)(2,1)S(1)} %collective-permute-done.14), channel_id=1, source_target_pairs={{0,480},{32,0},{64,32},{96,64},{128,96},{160,128},{192,160},{224,1... | collective-permute-start | bytes 393224 | tf_op jit(solution)/shard_map/ppermute | solution.py:24
  218.5 10.7 %collective-permute-start.17 = (bf16[256,256]{1,0:T(8,128)(2,1)S(1)}, bf16[256,256]{1,0:T(8,128)(2,1)S(1)}, u32[]{:S(2)}, u32[]{:S(2)}) collective-permute-start(bf16[256,256]{1,0:T(8,128)(2,1)S(1)} %collective-permute-done.15), channel_id=1, source_target_pairs={{0,32},{32,64},{64,96},{96,128},{128,160},{160,192},{192,224},{224... | collective-permute-start | bytes 393224 | tf_op jit(solution)/shard_map/ppermute | solution.py:19
  233.6 42.6 %copy-start.7 = (f32[256]{0:T(256)S(1)}, f32[256]{0:T(256)}, u32[]{:S(2)}) copy-start(f32[256]{0:T(256)} %copy-done.6) | copy-start | bytes 3076
  233.6 42.6 %copy-start.9 = (f32[256]{0:T(256)S(1)}, f32[256]{0:T(256)}, u32[]{:S(2)}) copy-start(f32[256]{0:T(256)} %copy-done.8) | copy-start | bytes 3076
  233.6 42.6 %copy-start.11 = (f32[256]{0:T(256)S(1)}, f32[256]{0:T(256)}, u32[]{:S(2)}) copy-start(f32[256]{0:T(256)} %copy-done.10) | copy-start | bytes 3076
  233.6 42.6 %copy-start.13 = (f32[256]{0:T(256)S(1)}, f32[256]{0:T(256)}, u32[]{:S(2)}) copy-start(f32[256]{0:T(256)} %copy-done.12) | copy-start | bytes 3076
  233.6 42.6 %copy-start.15 = (f32[256]{0:T(256)S(1)}, f32[256]{0:T(256)}, u32[]{:S(2)}) copy-start(f32[256]{0:T(256)} %copy-done.14) | copy-start | bytes 3076
  235.5 40.7 %collective-permute-start.2 = (f32[6,256]{1,0:T(8,128)S(1)}, f32[6,256]{1,0:T(8,128)S(1)}, u32[]{:S(2)}, u32[]{:S(2)}) collective-permute-start(f32[6,256]{1,0:T(8,128)S(1)} %slice.158), channel_id=1, source_target_pairs={{32,0},{64,32},{96,64},{128,96},{160,128},{192,160},{224,192},{256... | collective-permute-start | bytes 18440 | tf_op jit(solution)/shard_map/ppermute | solution.py:34
Sparse Core Ops, SparseCore 0:
  23.5 94.3 all-gather.2
  135.6 94.6 reduce-scatter.1
